TPU v7x, 256 devices: a whole 4x4x8 slice. The times are simulated.
256 devices in a mesh: expert: 128 (over y, x, z), dp: 2 (over core).
Axes of the slice: x: 4, y: 4, z: 8, core: 2. Of those that a mesh axis runs over, the one named last changes fastest.
Arguments:
- tokens: bfloat16 [32768, 2048], P(('expert', 'dp')), may hold values from -6 to 6
- out_grad: bfloat16 [32768, 2048], P(('expert', 'dp')), may hold values from -6 to 6
- gates: float32 [32768, 8], P(('expert', 'dp')), may hold values from 0.05 to 0.5
- expert_ids: int32 [32768, 8], P(('expert', 'dp')), may hold values from 0 to 127, all different within a row; in each aligned block of 128 rows (0 to 127, 128 to 255, ...) at most 10 rows name the same one
- w_gate: bfloat16 [128, 2048, 384], P('expert', 'dp'), may hold values from -0.125 to 0.125
- w_up: bfloat16 [128, 2048, 384], P('expert', 'dp'), may hold values from -0.125 to 0.125
- w_down: bfloat16 [128, 2048, 384], P('expert', 'dp'), may hold values from -0.3125 to 0.3125
Outputs:
- input_grad: bfloat16 [32768, 2048], P(('expert', 'dp'))
- grad_gate: float32 [128, 2048, 384], P('expert', 'dp')
- grad_up: float32 [128, 2048, 384], P('expert', 'dp')
- grad_down: float32 [128, 2048, 384], P('expert', 'dp')
Inputs may be any that keep to these rules, and one draw needn't show every extreme that they name: `expert_ids`: among the 128 tokens of one device no expert is named more than 10 times, and in every draw some device names some expert exactly 10 times. The ids of one token differ.
All inputs are finite; a program needn't handle non-finite values.
Results may differ from a plain program's by a relative error of at most 0.0065.
Values may be sent and summed in bfloat16 or wider, within the bound.
A program may use at most 128 MiB of HBM per device.

v0:
```python
import functools

import jax
import jax.numpy as jnp
from jax import lax
from jax.experimental import pallas as pl
from jax.experimental.pallas import tpu as pltpu
from jax.sharding import PartitionSpec as P

BF16 = jnp.bfloat16
F32 = jnp.float32
MESH = pl.DeviceIdType.MESH
ZS = 8
SUB = 8
GROUP = 4

OFFSET = (0, -1, 1, -2, 2, -3, 3, 4)
MAIN = (0, 1, 2, 3, 4, 6, 7, 8)
OVER = (5, 9)
CHUNKS = 10
SLOTS_OUT = 5

contract_rows = (((0,), (0,)), ((), ()))
contract_cols = (((1,), (1,)), ((), ()))


def kernel(lines, meta_ref, tok_ref, grad_ref, wg_ref, wu_ref, wd_ref,
           out_ref, gg_ref, gu_ref, gd_ref,
           meta, block_x, block_g, out_x, out_g, in_x, in_g, weights, acc, other_acc,
           pick_main, pick_over, gate_col, back, stage, buf,
           meta_send, meta_recv, zs_send, zs_recv, pl_send, pl_recv, rt_send, rt_recv,
           w_send, w_recv, a_send, a_recv, rs_send, rs_recv, own_sem):
    me = lax.axis_index("expert")
    core = lax.axis_index("dp")
    z, line = lax.rem(me, ZS), lax.div(me, ZS)
    toks, width = tok_ref.shape
    depth = wg_ref.shape[1]
    rows = lines * SUB
    half = width // 2

    def along_z(j):
        return {"expert": line * ZS + lax.rem(z + j + 2 * ZS, ZS)}

    def in_plane(other):
        return {"expert": other * ZS + z}

    sibling = {"dp": 1 - core}

    def send(src, dst, send_sem, recv_sem, device):
        return pltpu.make_async_remote_copy(
            src_ref=src, dst_ref=dst, send_sem=send_sem, recv_sem=recv_sem,
            device_id=device, device_id_type=MESH,
        )

    barrier = pltpu.get_barrier_semaphore()

    def greet_line(j, c):
        pl.semaphore_signal(barrier, inc=1, device_id=along_z(j), device_id_type=MESH)
        return c

    def greet_plane(d, c):
        pl.semaphore_signal(barrier, inc=1, device_id=in_plane(lax.rem(line + d, lines)), device_id_type=MESH)
        return c

    lax.fori_loop(1, ZS, greet_line, 0)
    lax.fori_loop(1, lines, greet_plane, 0)
    pl.semaphore_signal(barrier, inc=1, device_id=sibling, device_id_type=MESH)
    pl.semaphore_wait(barrier, ZS + lines - 1)

    sources = (tok_ref, grad_ref)
    gathered = (block_x, block_g)
    send_bufs = (out_x, out_g)
    recv_bufs = (in_x, in_g)

    def hop(t, src, dst, j):
        ref = sources[t] if src == 0 else gathered[t].at[src]
        return send(ref, gathered[t].at[dst], zs_send.at[t, dst], zs_recv.at[t, dst], along_z(j))

    own = [pltpu.make_async_copy(sources[t], gathered[t].at[0], own_sem.at[t]) for t in (0, 1)]
    metas = [send(meta_ref, meta.at[p], meta_send.at[p], meta_recv.at[p], along_z(-OFFSET[p])) for p in range(1, ZS)]
    for t in (0, 1):
        own[t].start()
        hop(t, 0, 1, 1).start()
        hop(t, 0, 2, -1).start()
    for m in metas:
        m.start()

    w_refs = (wg_ref, wu_ref, wd_ref)

    def mine(i):
        return weights.at[i, pl.ds(pl.multiple_of(core * depth, depth), depth)]

    w_remote = [send(w_refs[i].at[0], mine(i), w_send.at[i], w_recv.at[i], sibling) for i in range(3)]
    w_local = [pltpu.make_async_copy(w_refs[i].at[0], mine(i), own_sem.at[2 + i]) for i in range(3)]
    for i in range(3):
        w_remote[i].start()
        w_local[i].start()

    def iota(shape, axis):
        return lax.broadcasted_iota(jnp.int32, shape, axis)

    def ones_where(mask):
        return jnp.where(mask, 1.0, 0.0).astype(BF16)

    def prepare(p, c):
        m = meta[p]
        expert = (iota((lines, toks), 0) * ZS + z).astype(F32)
        named = jnp.zeros((lines, toks), F32)
        weight = jnp.zeros((lines, toks), F32)
        for k in range(8):
            hit = m[k : k + 1, :] == expert
            named = named + jnp.where(hit, 1.0, 0.0)
            weight = weight + jnp.where(hit, m[8 + k : 9 + k, :], 0.0)
        before = ones_where(iota((toks, toks), 0) < iota((toks, toks), 1))
        rank = jnp.dot(named.astype(BF16), before, preferred_element_type=F32)
        taken = named > 0
        shift = (lax.rem(p, GROUP) * 2).astype(F32) - SUB
        in_main = jnp.where(taken & (rank < SUB), rank, -1.0)
        in_over = jnp.where(taken & (rank >= SUB), rank + shift, -1.0)
        row = iota((rows, 1), 0)
        spread = ones_where(lax.div(row, SUB) == iota((rows, lines), 1))
        within = lax.rem(row, SUB).astype(F32)
        placed = jnp.dot(spread, jnp.concatenate([in_main, in_over], axis=1).astype(BF16), preferred_element_type=F32)
        main, over = placed[:, :toks] == within, placed[:, toks:] == within
        high = weight.astype(BF16)
        rest = weight - high.astype(F32)
        mid = rest.astype(BF16)
        low = (rest - mid.astype(F32)).astype(BF16)
        spread_w = jnp.dot(
            jnp.concatenate([spread, spread, spread], axis=1),
            jnp.concatenate([high, mid, low], axis=0),
            preferred_element_type=F32,
        )
        pick_main[p] = ones_where(main)
        pick_over[p] = ones_where(over)
        gate_col[p] = jnp.sum(jnp.where(main, spread_w, 0.0), axis=1, keepdims=True)
        at = ZS + lax.div(p, GROUP)
        gate_col[at] = gate_col[at] + jnp.sum(jnp.where(over, spread_w, 0.0), axis=1, keepdims=True)
        return c

    def chunk_send(t, k, d):
        other = lax.rem(line + d, lines)
        return send(send_bufs[t].at[k % SLOTS_OUT, other], recv_bufs[t].at[k, line], pl_send.at[t, k], pl_recv.at[t, k], in_plane(other))

    def sent(t, k):
        rest = send_bufs[t].at[k % SLOTS_OUT, pl.ds(0, lines - 1)]
        return pltpu.make_async_copy(rest, rest, pl_send.at[t, k])

    def route(k, places):
        for t in (0, 1):
            if k >= SLOTS_OUT:
                sent(t, k - SLOTS_OUT).wait()
            picks = pick_main if len(places) == 1 else pick_over
            total = None
            for p in places:
                part = jnp.dot(picks[p], gathered[t][p], preferred_element_type=F32)
                total = part if total is None else total + part
            if t == 1:
                total = total * gate_col[places[0] if len(places) == 1 else ZS + places[0] // GROUP]
            send_bufs[t][k % SLOTS_OUT] = total.reshape(lines, SUB, width).astype(BF16)

            def go(d, c, t=t):
                chunk_send(t, k, d).start()
                return c

            lax.fori_loop(1, lines, go, 0)
            pltpu.make_async_copy(send_bufs[t].at[k % SLOTS_OUT, line], recv_bufs[t].at[k, line], pl_recv.at[t, k]).start()

    def arrived(ref, sem):
        pltpu.make_async_copy(ref, ref, sem).wait()

    def expert(k):
        for t in (0, 1):
            arrived(recv_bufs[t].at[k], pl_recv.at[t, k])
        x = in_x[k].reshape(rows, width)
        dy = in_g[k].reshape(rows, width)
        gate_pre = jnp.dot(x, weights[0], preferred_element_type=F32)
        up_pre = jnp.dot(x, weights[1], preferred_element_type=F32)
        hidden_grad = jnp.dot(dy, weights[2], preferred_element_type=F32)
        sig = jax.nn.sigmoid(gate_pre)
        active = gate_pre * sig
        hidden = (active * up_pre).astype(BF16)
        gate_grad = (hidden_grad * up_pre * sig * (1.0 + gate_pre * (1.0 - sig))).astype(BF16)
        up_grad = (hidden_grad * active).astype(BF16)
        acc[0] += lax.dot_general(x, gate_grad, contract_rows, preferred_element_type=F32)
        acc[1] += lax.dot_general(x, up_grad, contract_rows, preferred_element_type=F32)
        acc[2] += lax.dot_general(dy, hidden, contract_rows, preferred_element_type=F32)
        row_grad = lax.dot_general(
            gate_grad, weights[0], contract_cols, preferred_element_type=F32
        ) + lax.dot_general(up_grad, weights[1], contract_cols, preferred_element_type=F32)
        in_x[k] = row_grad.reshape(lines, SUB, width).astype(BF16)

    def give_back(k):
        def go(d, c):
            other = lax.rem(line + d, lines)
            send(in_x.at[k, other], back.at[k, line], rt_send.at[k], rt_recv.at[k], in_plane(other)).start()
            return c

        lax.fori_loop(1, lines, go, 0)
        pltpu.make_async_copy(in_x.at[k, line], back.at[k, line], rt_recv.at[k]).start()

    gate_col[...] = jnp.zeros_like(gate_col)
    acc[...] = jnp.zeros_like(acc)
    meta[0] = meta_ref[...]
    prepare(0, 0)
    for t in (0, 1):
        own[t].wait()
    route(0, (0,))
    for m in metas:
        m.wait()
    lax.fori_loop(1, ZS, prepare, 0)

    def pass_on(t, src, dst, came, j):
        hop(t, came, src, j).wait()
        hop(t, src, dst, j).start()

    def work(k, c):
        @pl.when(k == 0)
        def _():
            for t in (0, 1):
                pass_on(t, 1, 3, 0, 1)
                pass_on(t, 2, 4, 0, -1)
            route(1, (1,))
            route(2, (2,))
            for i in range(3):
                w_local[i].wait()
                w_remote[i].wait()

        @pl.when(k == 1)
        def _():
            for t in (0, 1):
                pass_on(t, 3, 5, 1, 1)
                pass_on(t, 4, 6, 2, -1)
            route(3, (3,))
            route(4, (4,))
            route(5, (0, 1, 2, 3))

        @pl.when(k == 3)
        def _():
            pass_on(0, 5, 7, 3, 1)
            hop(0, 4, 6, -1).wait()
            hop(1, 3, 5, 1).wait()
            pass_on(1, 6, 7, 4, -1)
            route(6, (5,))
            route(7, (6,))

        @pl.when(k == 5)
        def _():
            hop(0, 5, 7, 1).wait()
            hop(1, 6, 7, -1).wait()
            route(8, (7,))
            route(9, (4, 5, 6, 7))

        expert(k)

        @pl.when((k == 4) | (k >= 6))
        def _():
            give_back(k)

        return c

    lax.fori_loop(0, CHUNKS, work, 0)
    for k in (5, 3, 2, 1, 0):
        give_back(k)

    def acc_rows(i, c):
        return acc.at[i, pl.ds(pl.multiple_of(c * depth, depth), depth)]

    acc_sends = [send(acc_rows(i, 1 - core), other_acc.at[i], a_send.at[i], a_recv.at[i], sibling) for i in range(3)]
    for s in acc_sends:
        s.start()

    def summed(p):
        return lax.dot_general(
            pick_main[p], back[MAIN[p]].reshape(rows, width), contract_rows, preferred_element_type=F32
        ) + lax.dot_general(
            pick_over[p], back[OVER[p // GROUP]].reshape(rows, width), contract_rows, preferred_element_type=F32
        )

    def returned(k):
        arrived(back.at[k], rt_recv.at[k])

    def ring(p, dst, j):
        return send(stage.at[p], buf.at[dst], rs_send.at[dst], rs_recv.at[dst], along_z(j))

    low, high = pl.ds(0, half), pl.ds(half, half)
    returned(9)
    returned(8)
    part = summed(7)
    stage[7] = part.astype(BF16)
    r4 = send(stage.at[7, :, low], buf.at[6, :, low], rs_send.at[6], rs_recv.at[6], along_z(1))
    l4 = send(stage.at[7, :, high], buf.at[5, :, high], rs_send.at[5], rs_recv.at[5], along_z(-1))
    r4.start()
    l4.start()
    returned(7)
    part = summed(6)
    r4.wait()
    stage[6, :, :half] = (part[:, :half] + buf[6, :, :half].astype(F32)).astype(BF16)
    stage[6, :, half:] = part[:, half:].astype(BF16)
    r3 = ring(6, 4, 1)
    r3.start()
    returned(6)
    part = summed(5)
    l4.wait()
    stage[5, :, :half] = part[:, :half].astype(BF16)
    stage[5, :, half:] = (part[:, half:] + buf[5, :, half:].astype(F32)).astype(BF16)
    l3 = ring(5, 3, -1)
    l3.start()

    outs = (gg_ref, gu_ref, gd_ref)
    stores = []
    for i in range(3):
        acc_sends[i].wait()
        other_acc[i] = other_acc[i] + acc[i, pl.ds(pl.multiple_of(core * depth, depth), depth), :]
        stores.append(pltpu.make_async_copy(other_acc.at[i], outs[i].at[0], own_sem.at[i]))
        stores[i].start()

    def forward(p, came):
        part = summed(p)
        came.wait()
        stage[p] = (part + buf[p].astype(F32)).astype(BF16)

    returned(4)
    forward(4, r3)
    r2 = ring(4, 2, 1)
    r2.start()
    returned(5)
    returned(3)
    forward(3, l3)
    l2 = ring(3, 1, -1)
    l2.start()
    returned(2)
    forward(2, r2)
    r1 = ring(2, 0, 1)
    r1.start()
    returned(1)
    forward(1, l2)
    l1 = ring(1, 7, -1)
    l1.start()
    returned(0)
    part = summed(0)
    r1.wait()
    l1.wait()
    out_ref[...] = (part + buf[0].astype(F32) + buf[7].astype(F32)).astype(BF16)

    for k in range(CHUNKS - SLOTS_OUT, CHUNKS):
        for t in (0, 1):
            sent(t, k).wait()
    for k in range(CHUNKS):
        rest = in_x.at[k, pl.ds(0, lines - 1)]
        arrived(rest, rt_send.at[k])
    for s in stores:
        s.wait()


def local(tokens, out_grad, gates, expert_ids, w_gate, w_up, w_down):
    lines = lax.axis_size("expert") // ZS
    toks, width = tokens.shape
    depth, ff = w_gate.shape[1:]
    rows = lines * SUB
    meta = jnp.concatenate([expert_ids.astype(F32).T, gates.T], axis=0)
    any_spec = pl.BlockSpec(memory_space=pl.ANY)
    vmem = pl.BlockSpec(memory_space=pltpu.VMEM)
    dma = pltpu.SemaphoreType.DMA
    grads = jax.ShapeDtypeStruct((1, depth, ff), F32)
    return pl.pallas_call(
        functools.partial(kernel, lines),
        out_shape=(jax.ShapeDtypeStruct((toks, width), BF16), grads, grads, grads),
        in_specs=[vmem] + [any_spec] * 5,
        out_specs=(vmem, any_spec, any_spec, any_spec),
        scratch_shapes=[
            pltpu.VMEM((ZS, 16, toks), F32),
            pltpu.VMEM((ZS, toks, width), BF16),
            pltpu.VMEM((ZS, toks, width), BF16),
            pltpu.VMEM((SLOTS_OUT, lines, SUB, width), BF16),
            pltpu.VMEM((SLOTS_OUT, lines, SUB, width), BF16),
            pltpu.VMEM((CHUNKS, lines, SUB, width), BF16),
            pltpu.VMEM((CHUNKS, lines, SUB, width), BF16),
            pltpu.VMEM((3, 2 * depth, ff), BF16),
            pltpu.VMEM((3, 2 * depth, ff), F32),
            pltpu.VMEM((3, depth, ff), F32),
            pltpu.VMEM((ZS, rows, toks), BF16),
            pltpu.VMEM((ZS, rows, toks), BF16),
            pltpu.VMEM((CHUNKS, rows, 1), F32),
            pltpu.VMEM((CHUNKS, lines, SUB, width), BF16),
            pltpu.VMEM((ZS, toks, width), BF16),
            pltpu.VMEM((ZS, toks, width), BF16),
            dma((ZS,)),
            dma((ZS,)),
            dma((2, ZS)),
            dma((2, ZS)),
            dma((2, CHUNKS)),
            dma((2, CHUNKS)),
            dma((CHUNKS,)),
            dma((CHUNKS,)),
            dma((3,)),
            dma((3,)),
            dma((3,)),
            dma((3,)),
            dma((ZS,)),
            dma((ZS,)),
            dma((5,)),
        ],
        compiler_params=pltpu.CompilerParams(
            collective_id=0, has_side_effects=True, vmem_limit_bytes=61 << 20
        ),
        name="experts_backward",
    )(meta, tokens, out_grad, w_gate, w_up, w_down)


def solution(mesh):
    rows = P(("expert", "dp"), None)
    weights = P("expert", "dp", None)
    return jax.shard_map(
        local,
        mesh=mesh,
        in_specs=(rows, rows, rows, rows, weights, weights, weights),
        out_specs=(rows, weights, weights, weights),
        check_vma=False,
    )
```

profile of v0, /device:TPU:16, one launch (start us, length us, event | category | flops | bytes accessed | tf_op | source)
XLA Modules:
  0.0 231.8 jit_solution(12978814290485653)
XLA Ops:
  0.6 0.7 convert_bitcast_fusion
  1.3 1.3 pad_maximum_fusion.meta_ref
  2.6 221.4 %experts_backward.1 = (bf16[128,2048]{1,0:T(8,128)(2,1)}, f32[1,1024,384]{2,1,0:T(8,128)}, f32[1,1024,384]{2,1,0:T(8,128)}, f32[1,1024,384]{2,1,0:T(8,128)}) custom-call(f32[16,128]{1,0:T(8,128)} %pad_maximum_fusion.meta_ref, bf16[128,2048]{1,0:T(8,128)(2,1)} %tok_ref.1, bf16[128,2048]{1,0:T(8,128)(2,1)} %grad_ref.1, bf16[1,1024,384]{2,1,0:T(8,128)(2,1)} %wg_ref.1, ...), custom_call_target="tpu_custom_call" | custom-call | tf_op jit(solution)/shard_map/experts_backward/pallas_call | solution.py:366
  224.0 1.9 copy.15
  225.9 0.0 copy-start.1
  225.9 2.8 %copy.16 = f32[1,1024,384]{2,1,0:T(8,128)} copy(f32[1,1024,384]{2,1,0:T(8,128)} %get-tuple-element.9) | data formatting | bytes 3145728
  228.7 0.0 copy-done.1
  228.7 0.0 copy-start
  228.7 1.1 copy.17
  229.9 0.8 copy-done
  230.7 1.1 copy.18
Async XLA Ops:
  225.9 2.8 %copy-start.1 = (f32[1,1024,384]{2,1,0:T(8,128)S(1)}, f32[1,1024,384]{2,1,0:T(8,128)}, u32[]{:S(2)}) copy-start(f32[1,1024,384]{2,1,0:T(8,128)} %get-tuple-element.10) | copy-start | bytes 4718596
  228.7 2.0 copy-start
where the time goes:
time: 234 us; the launch traced here: 232 us
  Pallas kernels  221 us (94%)
  local copies, waits for them, and re-layouts  7.77 us (3%)
    pallas_call x1, Pallas kernels, local(): pl.pallas_call(functools.partial(kernel, lines), out_shape=(jax.ShapeDtyp...  221 us
    unnamed x8, local copies, waits for them, and re-layouts  7.77 us

commit v1 on v0

--- a/solution.py
+++ b/solution.py
@@ -18,13 +18,13 @@
 MAIN = (0, 1, 2, 3, 4, 6, 7, 8)
 OVER = (5, 9)
 CHUNKS = 10
-SLOTS_OUT = 5
+SLOTS_OUT = 6
 
 contract_rows = (((0,), (0,)), ((), ()))
 contract_cols = (((1,), (1,)), ((), ()))
 
 
-def kernel(lines, meta_ref, tok_ref, grad_ref, wg_ref, wu_ref, wd_ref,
+def kernel(lines, ids_ref, gates_ref, tok_ref, grad_ref, wg_ref, wu_ref, wd_ref,
            out_ref, gg_ref, gu_ref, gd_ref,
            meta, block_x, block_g, out_x, out_g, in_x, in_g, weights, acc, other_acc,
            pick_main, pick_over, gate_col, back, stage, buf,
@@ -76,14 +76,23 @@
         ref = sources[t] if src == 0 else gathered[t].at[src]
         return send(ref, gathered[t].at[dst], zs_send.at[t, dst], zs_recv.at[t, dst], along_z(j))
 
+    def both_ways(t, right, left):
+        for (src, dst), j in ((right, 1), (left, -1)):
+            hop(t, src, dst, j).start()
+
+    def landed(t, right, left):
+        for (src, dst), j in ((right, 1), (left, -1)):
+            hop(t, src, dst, j).wait_recv()
+
     own = [pltpu.make_async_copy(sources[t], gathered[t].at[0], own_sem.at[t]) for t in (0, 1)]
-    metas = [send(meta_ref, meta.at[p], meta_send.at[p], meta_recv.at[p], along_z(-OFFSET[p])) for p in range(1, ZS)]
+    metas = [send(meta.at[0], meta.at[p], meta_send.at[p], meta_recv.at[p], along_z(-OFFSET[p])) for p in range(1, ZS)]
+    meta[0, :8] = ids_ref[...].astype(F32)
+    meta[0, 8:] = gates_ref[...]
+    for m in metas:
+        m.start()
+    both_ways(0, (0, 1), (0, 2))
     for t in (0, 1):
         own[t].start()
-        hop(t, 0, 1, 1).start()
-        hop(t, 0, 2, -1).start()
-    for m in metas:
-        m.start()
 
     w_refs = (wg_ref, wu_ref, wd_ref)
 
@@ -146,32 +155,32 @@
         rest = send_bufs[t].at[k % SLOTS_OUT, pl.ds(0, lines - 1)]
         return pltpu.make_async_copy(rest, rest, pl_send.at[t, k])
 
-    def route(k, places):
-        for t in (0, 1):
-            if k >= SLOTS_OUT:
-                sent(t, k - SLOTS_OUT).wait()
-            picks = pick_main if len(places) == 1 else pick_over
-            total = None
-            for p in places:
-                part = jnp.dot(picks[p], gathered[t][p], preferred_element_type=F32)
-                total = part if total is None else total + part
-            if t == 1:
-                total = total * gate_col[places[0] if len(places) == 1 else ZS + places[0] // GROUP]
-            send_bufs[t][k % SLOTS_OUT] = total.reshape(lines, SUB, width).astype(BF16)
-
-            def go(d, c, t=t):
-                chunk_send(t, k, d).start()
-                return c
-
-            lax.fori_loop(1, lines, go, 0)
-            pltpu.make_async_copy(send_bufs[t].at[k % SLOTS_OUT, line], recv_bufs[t].at[k, line], pl_recv.at[t, k]).start()
+    def route(t, k, places):
+        slot = k % SLOTS_OUT
+        if k >= SLOTS_OUT:
+            sent(t, k - SLOTS_OUT).wait()
+        picks = pick_main if len(places) == 1 else pick_over
+        total = None
+        for p in places:
+            part = jnp.dot(picks[p], gathered[t][p], preferred_element_type=F32)
+            total = part if total is None else total + part
+        if t == 1:
+            total = total * gate_col[places[0] if len(places) == 1 else ZS + places[0] // GROUP]
+        send_bufs[t][slot] = total.reshape(lines, SUB, width).astype(BF16)
+
+        def go(d, c):
+            chunk_send(t, k, d).start()
+            return c
+
+        lax.fori_loop(1, lines, go, 0)
+        recv_bufs[t][k, line] = send_bufs[t][slot, line]
 
     def arrived(ref, sem):
         pltpu.make_async_copy(ref, ref, sem).wait()
 
     def expert(k):
         for t in (0, 1):
-            arrived(recv_bufs[t].at[k], pl_recv.at[t, k])
+            arrived(recv_bufs[t].at[k, pl.ds(0, lines - 1)], pl_recv.at[t, k])
         x = in_x[k].reshape(rows, width)
         dy = in_g[k].reshape(rows, width)
         gate_pre = jnp.dot(x, weights[0], preferred_element_type=F32)
@@ -197,31 +206,28 @@
             return c
 
         lax.fori_loop(1, lines, go, 0)
-        pltpu.make_async_copy(in_x.at[k, line], back.at[k, line], rt_recv.at[k]).start()
+        back[k, line] = in_x[k, line]
 
     gate_col[...] = jnp.zeros_like(gate_col)
-    acc[...] = jnp.zeros_like(acc)
-    meta[0] = meta_ref[...]
     prepare(0, 0)
     for t in (0, 1):
         own[t].wait()
-    route(0, (0,))
+        route(t, 0, (0,))
+        if t == 0:
+            both_ways(1, (0, 1), (0, 2))
     for m in metas:
         m.wait()
     lax.fori_loop(1, ZS, prepare, 0)
-
-    def pass_on(t, src, dst, came, j):
-        hop(t, came, src, j).wait()
-        hop(t, src, dst, j).start()
+    acc[...] = jnp.zeros_like(acc)
 
     def work(k, c):
         @pl.when(k == 0)
         def _():
             for t in (0, 1):
-                pass_on(t, 1, 3, 0, 1)
-                pass_on(t, 2, 4, 0, -1)
-            route(1, (1,))
-            route(2, (2,))
+                landed(t, (0, 1), (0, 2))
+                both_ways(t, (1, 3), (2, 4))
+                route(t, 1, (1,))
+                route(t, 2, (2,))
             for i in range(3):
                 w_local[i].wait()
                 w_remote[i].wait()
@@ -229,39 +235,36 @@
         @pl.when(k == 1)
         def _():
             for t in (0, 1):
-                pass_on(t, 3, 5, 1, 1)
-                pass_on(t, 4, 6, 2, -1)
-            route(3, (3,))
-            route(4, (4,))
-            route(5, (0, 1, 2, 3))
+                landed(t, (1, 3), (2, 4))
+                both_ways(t, (3, 5), (4, 6))
+                route(t, 3, (3,))
+                route(t, 4, (4,))
+                route(t, 5, (0, 1, 2, 3))
 
         @pl.when(k == 3)
         def _():
-            pass_on(0, 5, 7, 3, 1)
-            hop(0, 4, 6, -1).wait()
-            hop(1, 3, 5, 1).wait()
-            pass_on(1, 6, 7, 4, -1)
-            route(6, (5,))
-            route(7, (6,))
-
-        @pl.when(k == 5)
+            for t in (0, 1):
+                landed(t, (3, 5), (4, 6))
+                (hop(0, 5, 7, 1) if t == 0 else hop(1, 6, 7, -1)).start()
+                route(t, 6, (5,))
+                route(t, 7, (6,))
+            for t in (0, 1):
+                (hop(0, 5, 7, 1) if t == 0 else hop(1, 6, 7, -1)).wait_recv()
+                route(t, 8, (7,))
+                route(t, 9, (4, 5, 6, 7))
+
+        expert(k)
+
+        @pl.when(k == 8)
         def _():
-            hop(0, 5, 7, 1).wait()
-            hop(1, 6, 7, -1).wait()
-            route(8, (7,))
-            route(9, (4, 5, 6, 7))
-
-        expert(k)
-
-        @pl.when((k == 4) | (k >= 6))
-        def _():
-            give_back(k)
+            give_back(7)
+            give_back(6)
 
         return c
 
     lax.fori_loop(0, CHUNKS, work, 0)
-    for k in (5, 3, 2, 1, 0):
-        give_back(k)
+    give_back(9)
+    give_back(8)
 
     def acc_rows(i, c):
         return acc.at[i, pl.ds(pl.multiple_of(c * depth, depth), depth)]
@@ -278,7 +281,7 @@
         )
 
     def returned(k):
-        arrived(back.at[k], rt_recv.at[k])
+        arrived(back.at[k, pl.ds(0, lines - 1)], rt_recv.at[k])
 
     def ring(p, dst, j):
         return send(stage.at[p], buf.at[dst], rs_send.at[dst], rs_recv.at[dst], along_z(j))
@@ -292,6 +295,8 @@
     l4 = send(stage.at[7, :, high], buf.at[5, :, high], rs_send.at[5], rs_recv.at[5], along_z(-1))
     r4.start()
     l4.start()
+    for k in (4, 5, 3, 2, 1, 0):
+        give_back(k)
     returned(7)
     part = summed(6)
     r4.wait()
@@ -343,8 +348,12 @@
     l1.wait()
     out_ref[...] = (part + buf[0].astype(F32) + buf[7].astype(F32)).astype(BF16)
 
-    for k in range(CHUNKS - SLOTS_OUT, CHUNKS):
-        for t in (0, 1):
+    for t in (0, 1):
+        for src, dst in ((0, 1), (1, 3), (3, 5)) + (((5, 7),) if t == 0 else ()):
+            hop(t, src, dst, 1).wait_send()
+        for src, dst in ((0, 2), (2, 4), (4, 6)) + (((6, 7),) if t == 1 else ()):
+            hop(t, src, dst, -1).wait_send()
+        for k in range(CHUNKS - SLOTS_OUT, CHUNKS):
             sent(t, k).wait()
     for k in range(CHUNKS):
         rest = in_x.at[k, pl.ds(0, lines - 1)]
@@ -353,20 +362,29 @@
         s.wait()
 
 
+def copies(*refs):
+    n = len(refs) // 2
+    sems = refs[-1]
+    moves = [pltpu.make_async_copy(refs[i], refs[n + i], sems.at[i]) for i in range(n)]
+    for m in moves:
+        m.start()
+    for m in moves:
+        m.wait()
+
+
 def local(tokens, out_grad, gates, expert_ids, w_gate, w_up, w_down):
     lines = lax.axis_size("expert") // ZS
     toks, width = tokens.shape
     depth, ff = w_gate.shape[1:]
     rows = lines * SUB
-    meta = jnp.concatenate([expert_ids.astype(F32).T, gates.T], axis=0)
     any_spec = pl.BlockSpec(memory_space=pl.ANY)
     vmem = pl.BlockSpec(memory_space=pltpu.VMEM)
     dma = pltpu.SemaphoreType.DMA
     grads = jax.ShapeDtypeStruct((1, depth, ff), F32)
-    return pl.pallas_call(
+    results = pl.pallas_call(
         functools.partial(kernel, lines),
         out_shape=(jax.ShapeDtypeStruct((toks, width), BF16), grads, grads, grads),
-        in_specs=[vmem] + [any_spec] * 5,
+        in_specs=[vmem] * 2 + [any_spec] * 5,
         out_specs=(vmem, any_spec, any_spec, any_spec),
         scratch_shapes=[
             pltpu.VMEM((ZS, 16, toks), F32),
@@ -405,7 +423,15 @@
             collective_id=0, has_side_effects=True, vmem_limit_bytes=61 << 20
         ),
         name="experts_backward",
-    )(meta, tokens, out_grad, w_gate, w_up, w_down)
+    )(expert_ids.T, gates.T, tokens, out_grad, w_gate, w_up, w_down)
+    return pl.pallas_call(
+        copies,
+        out_shape=tuple(jax.ShapeDtypeStruct(r.shape, r.dtype) for r in results),
+        in_specs=[any_spec] * 4,
+        out_specs=(any_spec,) * 4,
+        scratch_shapes=[dma((4,))],
+        name="results",
+    )(*results)
 
 
 def solution(mesh):

time: 234 us -> 367 us (1.57)
  Pallas kernels: 221 us -> 365 us
  local copies, waits for them, and re-layouts: 7.77 us -> 0 us
    pallas_call x0 -> x1, Pallas kernels: none -> 160 us  [local(): pl.pallas_call(copies, out_shape=tuple((jax.ShapeDtypeStruct(r.shape, r.d...]
    pallas_call x1, Pallas kernels: 221 us -> 205 us  [local(): pl.pallas_call(functools.partial(kernel, lines), out_shape=(jax.ShapeDtyp...]
    unnamed x8 -> x0, local copies, waits for them, and re-layouts: 7.77 us -> none
where the time goes in v1:
time: 367 us; the launch traced here: 366 us
  Pallas kernels  365 us (99%)
    pallas_call x1, Pallas kernels, local(): pl.pallas_call(functools.partial(kernel, lines), out_shape=(jax.ShapeDtyp...  205 us
    pallas_call x1, Pallas kernels, local(): pl.pallas_call(copies, out_shape=tuple((jax.ShapeDtypeStruct(r.shape, r.d...  160 us

profile of v1, /device:TPU:16, one launch (start us, length us, event | category | flops | bytes accessed | tf_op | source)
XLA Modules:
  0.0 365.7 jit_solution(2613513539352921445)
XLA Ops:
  0.6 204.9 %experts_backward.1 = (bf16[128,2048]{1,0:T(8,128)(2,1)}, f32[1,1024,384]{2,1,0:T(8,128)}, f32[1,1024,384]{2,1,0:T(8,128)}, f32[1,1024,384]{2,1,0:T(8,128)}) custom-call(s32[8,128]{1,0:T(8,128)} %bitcast.2, f32[8,128]{1,0:T(8,128)} %bitcast.3, bf16[128,2048]{1,0:T(8,128)(2,1)} %tok_ref.1, bf16[128,2048]{1,0:T(8,128)(2,1)} %grad_ref.1, ...), custom_call_target="tpu_custom_call" | custom-call | tf_op jit(solution)/shard_map/experts_backward/pallas_call | solution.py:384
  205.6 160.0 %results.1 = (bf16[128,2048]{1,0:T(8,128)(2,1)}, f32[1,1024,384]{2,1,0:T(8,128)}, f32[1,1024,384]{2,1,0:T(8,128)}, f32[1,1024,384]{2,1,0:T(8,128)}) custom-call(bf16[128,2048]{1,0:T(8,128)(2,1)} %get-tuple-element.8.refs_0_, f32[1,1024,384]{2,1,0:T(8,128)} %get-tuple-element.9.refs_1_, f32[1,1024,384]{2,1,0:T(8,128)} %get-tuple-element.10.refs_2_, ...), custom_call_target="tpu_custom_call" | custom-call | tf_op jit(solution)/shard_map/results/pallas_call | solution.py:427

commit v2 on v1

--- a/solution.py
+++ b/solution.py
@@ -19,6 +19,7 @@
 OVER = (5, 9)
 CHUNKS = 10
 SLOTS_OUT = 6
+PIECES = 4
 
 contract_rows = (((0,), (0,)), ((), ()))
 contract_cols = (((1,), (1,)), ((), ()))
@@ -65,7 +66,6 @@
     lax.fori_loop(1, ZS, greet_line, 0)
     lax.fori_loop(1, lines, greet_plane, 0)
     pl.semaphore_signal(barrier, inc=1, device_id=sibling, device_id_type=MESH)
-    pl.semaphore_wait(barrier, ZS + lines - 1)
 
     sources = (tok_ref, grad_ref)
     gathered = (block_x, block_g)
@@ -88,11 +88,12 @@
     metas = [send(meta.at[0], meta.at[p], meta_send.at[p], meta_recv.at[p], along_z(-OFFSET[p])) for p in range(1, ZS)]
     meta[0, :8] = ids_ref[...].astype(F32)
     meta[0, 8:] = gates_ref[...]
+    for t in (0, 1):
+        own[t].start()
+    pl.semaphore_wait(barrier, ZS + lines - 1)
+    both_ways(0, (0, 1), (0, 2))
     for m in metas:
         m.start()
-    both_ways(0, (0, 1), (0, 2))
-    for t in (0, 1):
-        own[t].start()
 
     w_refs = (wg_ref, wu_ref, wd_ref)
 
@@ -102,7 +103,6 @@
     w_remote = [send(w_refs[i].at[0], mine(i), w_send.at[i], w_recv.at[i], sibling) for i in range(3)]
     w_local = [pltpu.make_async_copy(w_refs[i].at[0], mine(i), own_sem.at[2 + i]) for i in range(3)]
     for i in range(3):
-        w_remote[i].start()
         w_local[i].start()
 
     def iota(shape, axis):
@@ -229,17 +229,16 @@
                 route(t, 1, (1,))
                 route(t, 2, (2,))
             for i in range(3):
-                w_local[i].wait()
-                w_remote[i].wait()
-
-        @pl.when(k == 1)
-        def _():
+                w_remote[i].start()
             for t in (0, 1):
                 landed(t, (1, 3), (2, 4))
                 both_ways(t, (3, 5), (4, 6))
                 route(t, 3, (3,))
                 route(t, 4, (4,))
                 route(t, 5, (0, 1, 2, 3))
+            for i in range(3):
+                w_local[i].wait()
+                w_remote[i].wait()
 
         @pl.when(k == 3)
         def _():
@@ -363,13 +362,22 @@
 
 
 def copies(*refs):
-    n = len(refs) // 2
-    sems = refs[-1]
-    moves = [pltpu.make_async_copy(refs[i], refs[n + i], sems.at[i]) for i in range(n)]
-    for m in moves:
-        m.start()
-    for m in moves:
-        m.wait()
+    n = 4
+    came, left, held, sems = refs[:n], refs[n : 2 * n], refs[2 * n : 3 * n], refs[3 * n]
+    parts = [(i, j) for j in range(PIECES) for i in range(n)]
+
+    def move(src, dst, i, j, way):
+        size = src[i].shape[-2] // PIECES
+        at = (0,) * (len(src[i].shape) - 2) + (pl.ds(j * size, size),)
+        return pltpu.make_async_copy(src[i].at[at], dst[i].at[at], sems.at[way, i, j])
+
+    for i, j in parts:
+        move(came, held, i, j, 0).start()
+    for i, j in parts:
+        move(came, held, i, j, 0).wait()
+        move(held, left, i, j, 1).start()
+    for i, j in parts:
+        move(held, left, i, j, 1).wait()
 
 
 def local(tokens, out_grad, gates, expert_ids, w_gate, w_up, w_down):
@@ -429,7 +437,8 @@
         out_shape=tuple(jax.ShapeDtypeStruct(r.shape, r.dtype) for r in results),
         in_specs=[any_spec] * 4,
         out_specs=(any_spec,) * 4,
-        scratch_shapes=[dma((4,))],
+        scratch_shapes=[pltpu.VMEM(r.shape, r.dtype) for r in results] + [dma((2, 4, PIECES))],
+        compiler_params=pltpu.CompilerParams(vmem_limit_bytes=60 << 20),
         name="results",
     )(*results)
 

time: 367 us -> 214 us (0.58)
  the two profiles are of different devices: /device:TPU:16 before, /device:TPU:6 now
where the time goes in v2:
time: 214 us
  Pallas kernels  213 us (100%)
    pallas_call x1, Pallas kernels, local(): pl.pallas_call(functools.partial(kernel, lines), out_shape=(jax.ShapeDtyp...  208 us
    pallas_call x1, Pallas kernels, local(): pl.pallas_call(copies, out_shape=tuple((jax.ShapeDtypeStruct(r.shape, r.d...  4.96 us

profile of v2, /device:TPU:6, one launch (start us, length us, event | category | flops | bytes accessed | tf_op | source)
XLA Modules:
  0.0 214.1 jit_solution(6031085049649400029)
XLA Ops:
  0.6 208.3 %experts_backward.1 = (bf16[128,2048]{1,0:T(8,128)(2,1)}, f32[1,1024,384]{2,1,0:T(8,128)}, f32[1,1024,384]{2,1,0:T(8,128)}, f32[1,1024,384]{2,1,0:T(8,128)}) custom-call(s32[8,128]{1,0:T(8,128)} %bitcast.2, f32[8,128]{1,0:T(8,128)} %bitcast.3, bf16[128,2048]{1,0:T(8,128)(2,1)} %tok_ref.1, bf16[128,2048]{1,0:T(8,128)(2,1)} %grad_ref.1, ...), custom_call_target="tpu_custom_call" | custom-call | tf_op jit(solution)/shard_map/experts_backward/pallas_call | solution.py:392
  208.9 5.0 %results.1 = (bf16[128,2048]{1,0:T(8,128)(2,1)}, f32[1,1024,384]{2,1,0:T(8,128)}, f32[1,1024,384]{2,1,0:T(8,128)}, f32[1,1024,384]{2,1,0:T(8,128)}) custom-call(bf16[128,2048]{1,0:T(8,128)(2,1)} %get-tuple-element.8.refs_0_, f32[1,1024,384]{2,1,0:T(8,128)} %get-tuple-element.9.refs_1_, f32[1,1024,384]{2,1,0:T(8,128)} %get-tuple-element.10.refs_2_, ...), custom_call_target="tpu_custom_call" | custom-call | tf_op jit(solution)/shard_map/results/pallas_call | solution.py:435

commit v3 on v2

--- a/solution.py
+++ b/solution.py
@@ -15,8 +15,8 @@
 GROUP = 4
 
 OFFSET = (0, -1, 1, -2, 2, -3, 3, 4)
-MAIN = (0, 1, 2, 3, 4, 6, 7, 8)
-OVER = (5, 9)
+MAIN = (0, 1, 2, 3, 4, 5, 6, 7)
+OVER = (9, 8)
 CHUNKS = 10
 SLOTS_OUT = 6
 PIECES = 4
@@ -90,11 +90,6 @@
     meta[0, 8:] = gates_ref[...]
     for t in (0, 1):
         own[t].start()
-    pl.semaphore_wait(barrier, ZS + lines - 1)
-    both_ways(0, (0, 1), (0, 2))
-    for m in metas:
-        m.start()
-
     w_refs = (wg_ref, wu_ref, wd_ref)
 
     def mine(i):
@@ -147,6 +142,14 @@
         gate_col[at] = gate_col[at] + jnp.sum(jnp.where(over, spread_w, 0.0), axis=1, keepdims=True)
         return c
 
+    gate_col[...] = jnp.zeros_like(gate_col)
+    prepare(0, 0)
+
+    pl.semaphore_wait(barrier, ZS + lines - 1)
+    both_ways(0, (0, 1), (0, 2))
+    for m in metas:
+        m.start()
+
     def chunk_send(t, k, d):
         other = lax.rem(line + d, lines)
         return send(send_bufs[t].at[k % SLOTS_OUT, other], recv_bufs[t].at[k, line], pl_send.at[t, k], pl_recv.at[t, k], in_plane(other))
@@ -208,8 +211,6 @@
         lax.fori_loop(1, lines, go, 0)
         back[k, line] = in_x[k, line]
 
-    gate_col[...] = jnp.zeros_like(gate_col)
-    prepare(0, 0)
     for t in (0, 1):
         own[t].wait()
         route(t, 0, (0,))
@@ -235,7 +236,6 @@
                 both_ways(t, (3, 5), (4, 6))
                 route(t, 3, (3,))
                 route(t, 4, (4,))
-                route(t, 5, (0, 1, 2, 3))
             for i in range(3):
                 w_local[i].wait()
                 w_remote[i].wait()
@@ -245,25 +245,27 @@
             for t in (0, 1):
                 landed(t, (3, 5), (4, 6))
                 (hop(0, 5, 7, 1) if t == 0 else hop(1, 6, 7, -1)).start()
-                route(t, 6, (5,))
-                route(t, 7, (6,))
+                route(t, 5, (5,))
+                route(t, 6, (6,))
             for t in (0, 1):
                 (hop(0, 5, 7, 1) if t == 0 else hop(1, 6, 7, -1)).wait_recv()
-                route(t, 8, (7,))
-                route(t, 9, (4, 5, 6, 7))
+                route(t, 7, (7,))
+                route(t, 8, (4, 5, 6, 7))
+            for t in (0, 1):
+                route(t, 9, (0, 1, 2, 3))
 
         expert(k)
 
         @pl.when(k == 8)
         def _():
             give_back(7)
-            give_back(6)
+            give_back(8)
 
         return c
 
     lax.fori_loop(0, CHUNKS, work, 0)
-    give_back(9)
-    give_back(8)
+    give_back(6)
+    give_back(5)
 
     def acc_rows(i, c):
         return acc.at[i, pl.ds(pl.multiple_of(c * depth, depth), depth)]
@@ -286,24 +288,24 @@
         return send(stage.at[p], buf.at[dst], rs_send.at[dst], rs_recv.at[dst], along_z(j))
 
     low, high = pl.ds(0, half), pl.ds(half, half)
-    returned(9)
     returned(8)
+    returned(7)
     part = summed(7)
     stage[7] = part.astype(BF16)
     r4 = send(stage.at[7, :, low], buf.at[6, :, low], rs_send.at[6], rs_recv.at[6], along_z(1))
     l4 = send(stage.at[7, :, high], buf.at[5, :, high], rs_send.at[5], rs_recv.at[5], along_z(-1))
     r4.start()
     l4.start()
-    for k in (4, 5, 3, 2, 1, 0):
+    for k in (4, 9, 3, 2, 1, 0):
         give_back(k)
-    returned(7)
+    returned(6)
     part = summed(6)
     r4.wait()
     stage[6, :, :half] = (part[:, :half] + buf[6, :, :half].astype(F32)).astype(BF16)
     stage[6, :, half:] = part[:, half:].astype(BF16)
     r3 = ring(6, 4, 1)
     r3.start()
-    returned(6)
+    returned(5)
     part = summed(5)
     l4.wait()
     stage[5, :, :half] = part[:, :half].astype(BF16)
@@ -328,7 +330,7 @@
     forward(4, r3)
     r2 = ring(4, 2, 1)
     r2.start()
-    returned(5)
+    returned(9)
     returned(3)
     forward(3, l3)
     l2 = ring(3, 1, -1)

time: 214 us -> 208 us (0.972)
  the two profiles are of different devices: /device:TPU:6 before, /device:TPU:16 now
where the time goes in v3:
time: 208 us
  Pallas kernels  207 us (100%)
    pallas_call x1, Pallas kernels, local(): pl.pallas_call(functools.partial(kernel, lines), out_shape=(jax.ShapeDtyp...  202 us
    pallas_call x1, Pallas kernels, local(): pl.pallas_call(copies, out_shape=tuple((jax.ShapeDtypeStruct(r.shape, r.d...  4.96 us

profile of v3, /device:TPU:16, one launch (start us, length us, event | category | flops | bytes accessed | tf_op | source)
XLA Modules:
  0.0 208.2 jit_solution(9081979384961514813)
XLA Ops:
  0.6 202.4 %experts_backward.1 = (bf16[128,2048]{1,0:T(8,128)(2,1)}, f32[1,1024,384]{2,1,0:T(8,128)}, f32[1,1024,384]{2,1,0:T(8,128)}, f32[1,1024,384]{2,1,0:T(8,128)}) custom-call(s32[8,128]{1,0:T(8,128)} %bitcast.2, f32[8,128]{1,0:T(8,128)} %bitcast.3, bf16[128,2048]{1,0:T(8,128)(2,1)} %tok_ref.1, bf16[128,2048]{1,0:T(8,128)(2,1)} %grad_ref.1, ...), custom_call_target="tpu_custom_call" | custom-call | tf_op jit(solution)/shard_map/experts_backward/pallas_call | solution.py:394
  203.1 5.0 %results.1 = (bf16[128,2048]{1,0:T(8,128)(2,1)}, f32[1,1024,384]{2,1,0:T(8,128)}, f32[1,1024,384]{2,1,0:T(8,128)}, f32[1,1024,384]{2,1,0:T(8,128)}) custom-call(bf16[128,2048]{1,0:T(8,128)(2,1)} %get-tuple-element.8.refs_0_, f32[1,1024,384]{2,1,0:T(8,128)} %get-tuple-element.9.refs_1_, f32[1,1024,384]{2,1,0:T(8,128)} %get-tuple-element.10.refs_2_, ...), custom_call_target="tpu_custom_call" | custom-call | tf_op jit(solution)/shard_map/results/pallas_call | solution.py:437

commit v4 on v3

--- a/solution.py
+++ b/solution.py
@@ -218,8 +218,7 @@
             both_ways(1, (0, 1), (0, 2))
     for m in metas:
         m.wait()
-    lax.fori_loop(1, ZS, prepare, 0)
-    acc[...] = jnp.zeros_like(acc)
+    lax.fori_loop(1, 3, prepare, 0)
 
     def work(k, c):
         @pl.when(k == 0)
@@ -229,8 +228,11 @@
                 both_ways(t, (1, 3), (2, 4))
                 route(t, 1, (1,))
                 route(t, 2, (2,))
+                if t == 0:
+                    lax.fori_loop(3, ZS, prepare, 0)
             for i in range(3):
                 w_remote[i].start()
+            acc[...] = jnp.zeros_like(acc)
             for t in (0, 1):
                 landed(t, (1, 3), (2, 4))
                 both_ways(t, (3, 5), (4, 6))
@@ -247,6 +249,9 @@
                 (hop(0, 5, 7, 1) if t == 0 else hop(1, 6, 7, -1)).start()
                 route(t, 5, (5,))
                 route(t, 6, (6,))
+
+        @pl.when(k == 4)
+        def _():
             for t in (0, 1):
                 (hop(0, 5, 7, 1) if t == 0 else hop(1, 6, 7, -1)).wait_recv()
                 route(t, 7, (7,))
@@ -271,8 +276,6 @@
         return acc.at[i, pl.ds(pl.multiple_of(c * depth, depth), depth)]
 
     acc_sends = [send(acc_rows(i, 1 - core), other_acc.at[i], a_send.at[i], a_recv.at[i], sibling) for i in range(3)]
-    for s in acc_sends:
-        s.start()
 
     def summed(p):
         return lax.dot_general(
@@ -298,6 +301,8 @@
     l4.start()
     for k in (4, 9, 3, 2, 1, 0):
         give_back(k)
+    for s in acc_sends:
+        s.start()
     returned(6)
     part = summed(6)
     r4.wait()
@@ -312,14 +317,6 @@
     stage[5, :, half:] = (part[:, half:] + buf[5, :, half:].astype(F32)).astype(BF16)
     l3 = ring(5, 3, -1)
     l3.start()
-
-    outs = (gg_ref, gu_ref, gd_ref)
-    stores = []
-    for i in range(3):
-        acc_sends[i].wait()
-        other_acc[i] = other_acc[i] + acc[i, pl.ds(pl.multiple_of(core * depth, depth), depth), :]
-        stores.append(pltpu.make_async_copy(other_acc.at[i], outs[i].at[0], own_sem.at[i]))
-        stores[i].start()
 
     def forward(p, came):
         part = summed(p)
@@ -343,6 +340,13 @@
     forward(1, l2)
     l1 = ring(1, 7, -1)
     l1.start()
+    outs = (gg_ref, gu_ref, gd_ref)
+    stores = []
+    for i in range(3):
+        acc_sends[i].wait()
+        other_acc[i] = other_acc[i] + acc[i, pl.ds(pl.multiple_of(core * depth, depth), depth), :]
+        stores.append(pltpu.make_async_copy(other_acc.at[i], outs[i].at[0], own_sem.at[i]))
+        stores[i].start()
     returned(0)
     part = summed(0)
     r1.wait()

time: 208 us -> 205 us (0.986)
  Pallas kernels: 207 us -> 203 us
    pallas_call x1, Pallas kernels: 202 us -> 198 us  [local(): pl.pallas_call(functools.partial(kernel, lines), out_shape=(jax.ShapeDtyp...]
where the time goes in v4:
time: 205 us; the launch traced here: 203 us
  Pallas kernels  203 us (99%)
    pallas_call x1, Pallas kernels, local(): pl.pallas_call(functools.partial(kernel, lines), out_shape=(jax.ShapeDtyp...  198 us
    pallas_call x1, Pallas kernels, local(): pl.pallas_call(copies, out_shape=tuple((jax.ShapeDtypeStruct(r.shape, r.d...  4.96 us

profile of v4, /device:TPU:16, one launch (start us, length us, event | category | flops | bytes accessed | tf_op | source)
XLA Modules:
  0.0 203.5 jit_solution(1279853139019283548)
XLA Ops:
  0.6 197.7 %experts_backward.1 = (bf16[128,2048]{1,0:T(8,128)(2,1)}, f32[1,1024,384]{2,1,0:T(8,128)}, f32[1,1024,384]{2,1,0:T(8,128)}, f32[1,1024,384]{2,1,0:T(8,128)}) custom-call(s32[8,128]{1,0:T(8,128)} %bitcast.2, f32[8,128]{1,0:T(8,128)} %bitcast.3, bf16[128,2048]{1,0:T(8,128)(2,1)} %tok_ref.1, bf16[128,2048]{1,0:T(8,128)(2,1)} %grad_ref.1, ...), custom_call_target="tpu_custom_call" | custom-call | tf_op jit(solution)/shard_map/experts_backward/pallas_call | solution.py:398
  198.3 5.0 %results.1 = (bf16[128,2048]{1,0:T(8,128)(2,1)}, f32[1,1024,384]{2,1,0:T(8,128)}, f32[1,1024,384]{2,1,0:T(8,128)}, f32[1,1024,384]{2,1,0:T(8,128)}) custom-call(bf16[128,2048]{1,0:T(8,128)(2,1)} %get-tuple-element.8.refs_0_, f32[1,1024,384]{2,1,0:T(8,128)} %get-tuple-element.9.refs_1_, f32[1,1024,384]{2,1,0:T(8,128)} %get-tuple-element.10.refs_2_, ...), custom_call_target="tpu_custom_call" | custom-call | tf_op jit(solution)/shard_map/results/pallas_call | solution.py:441
